TPU v7x, 512 devices: a whole 4x8x8 slice. The times are simulated.
512 devices in a mesh: cam: 8 (over y_lo, x), sp: 64 (over z, y_hi, core).
Axes of the slice: x: 4, y: 8 (y_hi: 4, y_lo: 2; y = y_hi * 2 + y_lo), z: 8, core: 2. Of those that a mesh axis runs over, the one named last changes fastest.
Arguments:
- q_self: bfloat16 [8, 2048, 2048], P('cam', 'sp'), may hold values from -8 to 8
- keys: bfloat16 [8, 2048, 2048], P('cam', 'sp'), may hold values from -4 to 4
- values: bfloat16 [8, 2048, 2048], P('cam', 'sp'), may hold values from -4 to 4
- q_cross: bfloat16 [8, 2048, 2048], P('cam', 'sp'), may hold values from -8 to 8
- timestep: int32 [1], replicated, may hold values from 0 to 49
- mod_table: float32 [50, 2, 2048], replicated, may hold values from 0.5 to 3
Outputs:
- block_out: bfloat16 [8, 2048, 2048], P('cam', 'sp')
All inputs are finite; a program needn't handle non-finite values.
Results may differ from a plain program's by a relative error of at most 0.0042.
Values may be sent and summed in bfloat16 or wider, within the bound.
No kernel may reach another device: no remote copies, remote signals or barrier semaphores. Data moves between devices by JAX's collectives and lax.ppermute only.
A program may use at most 64 MiB of HBM per device.

v0:
```python
import math
import jax
import jax.numpy as jnp
from jax import lax
from jax.sharding import PartitionSpec as P

HEADS = 16


def passed_along(value, axis, steps):
    count = lax.axis_size(axis)
    pairs = [(source, (source + steps) % count) for source in range(count)]
    return lax.ppermute(value, axis, pairs)


def pick_block(extent, ceiling):
    block_size = min(ceiling, extent)
    while extent % block_size:
        block_size = block_size - 1
    return block_size


def attend(queries, key_rows, value_rows, score_scale):
    query_count, head_dim = queries.shape
    key_count = key_rows.shape[0]
    query_block = pick_block(query_count, 512)
    key_block = pick_block(key_count, 1024)
    key_blocks = key_rows.reshape(key_count // key_block, key_block, head_dim)
    value_blocks = value_rows.reshape(key_count // key_block, key_block, head_dim)

    def per_query(query_part):

        def absorb(state_now, pair_now):
            numerator, runmax, totals = state_now
            key_part, value_part = pair_now
            scores = (
                jnp.einsum("qd,kd->qk", query_part, key_part, preferred_element_type=jnp.float32)
                * score_scale
            )
            newmax = jnp.maximum(runmax, jnp.max(scores, axis=1))
            factor = jnp.exp(runmax - newmax)
            weights = jnp.exp(scores - newmax[:, None])
            totals = totals * factor + jnp.sum(weights, axis=1)
            numerator = numerator * factor[:, None] + jnp.dot(
                weights.astype(jnp.bfloat16), value_part, preferred_element_type=jnp.float32
            )
            return ((numerator, newmax, totals), None)

        start_state = (
            jnp.zeros((query_block, head_dim), jnp.float32),
            jnp.full((query_block,), -jnp.inf, jnp.float32),
            jnp.zeros((query_block,), jnp.float32),
        )
        final_state, _ = lax.scan(absorb, start_state, (key_blocks, value_blocks))
        return final_state

    numerator, runmax, totals = lax.map(
        per_query, queries.reshape(query_count // query_block, query_block, head_dim)
    )
    return (
        numerator.reshape(query_count, head_dim),
        runmax.reshape(query_count),
        totals.reshape(query_count),
    )


def local(q_self, keys, values, q_cross, timestep, mod_table):
    row_count = q_self.shape[1]
    full_width = q_self.shape[2]
    head_count = HEADS
    head_dim = full_width // head_count
    groups = lax.axis_size("sp")
    copies = groups // head_count
    part_rows = row_count // copies
    score_scale = 1.0 / math.sqrt(head_dim)
    query_heads = q_self[0].reshape(row_count, head_count, head_dim)
    key_heads = keys[0].reshape(row_count, head_count, head_dim)
    value_heads = values[0].reshape(row_count, head_count, head_dim)

    def quartered(tensor):
        return (
            tensor.reshape(copies, part_rows, head_count, head_dim)
            .transpose(2, 0, 1, 3)
            .reshape(groups, part_rows, head_dim)
        )

    spread = jnp.broadcast_to(
        query_heads.transpose(1, 0, 2)[:, None], (head_count, copies, row_count, head_dim)
    )
    queries_here = lax.all_to_all(
        spread.reshape(groups, row_count, head_dim), "sp", split_axis=0, concat_axis=1, tiled=True
    )
    keys_here = lax.all_to_all(quartered(key_heads), "sp", split_axis=0, concat_axis=1, tiled=True)
    values_here = lax.all_to_all(
        quartered(value_heads), "sp", split_axis=0, concat_axis=1, tiled=True
    )
    numerator, runmax, totals = attend(queries_here[0], keys_here[0], values_here[0], score_scale)
    numerator, runmax, totals = (
        lax.all_to_all(
            numerator.reshape(groups, row_count, head_dim),
            "sp",
            split_axis=0,
            concat_axis=0,
            tiled=True,
        ),
        lax.all_to_all(
            runmax.reshape(groups, row_count), "sp", split_axis=0, concat_axis=0, tiled=True
        ),
        lax.all_to_all(
            totals.reshape(groups, row_count), "sp", split_axis=0, concat_axis=0, tiled=True
        ),
    )
    numerator = numerator.reshape(head_count, copies, row_count, head_dim)
    runmax = runmax.reshape(head_count, copies, row_count)
    totals = totals.reshape(head_count, copies, row_count)
    topmax = jnp.max(runmax, axis=1)
    factor = jnp.exp(runmax - topmax[:, None])
    numerator = jnp.sum(numerator * factor[..., None], axis=1)
    totals = jnp.sum(totals * factor, axis=1)
    self_out = (
        (numerator / totals[..., None])
        .astype(jnp.bfloat16)
        .transpose(1, 0, 2)
        .reshape(row_count, full_width)
    )
    left_keys, left_values = passed_along((keys[0], values[0]), "cam", 1)
    right_keys, right_values = passed_along((keys[0], values[0]), "cam", -1)
    near_keys = jnp.concatenate([left_keys, right_keys], axis=0).reshape(
        2 * row_count, head_count, head_dim
    )
    near_values = jnp.concatenate([left_values, right_values], axis=0).reshape(
        2 * row_count, head_count, head_dim
    )
    cross_queries = q_cross[0].reshape(row_count, head_count, head_dim)
    scores = (
        jnp.einsum("qhd,khd->hqk", cross_queries, near_keys, preferred_element_type=jnp.float32)
        * score_scale
    )
    row_peak = jnp.max(scores, axis=2)
    weights = jnp.exp(scores - row_peak[..., None])
    totals = jnp.sum(weights, axis=2)
    numerator = jnp.einsum(
        "hqk,khd->qhd",
        weights.astype(jnp.bfloat16),
        near_values,
        preferred_element_type=jnp.float32,
    )
    cross_out = (numerator / totals.T[:, :, None]).reshape(row_count, full_width)
    selector = (jnp.arange(mod_table.shape[0]) == timestep[0]).astype(jnp.float32)
    gate_rows = jnp.tensordot(selector, mod_table, axes=1, precision=lax.Precision.HIGHEST)
    mixed = gate_rows[0] * self_out.astype(jnp.float32) + gate_rows[1] * cross_out
    return mixed.astype(jnp.bfloat16)[None]


def solution(mesh):
    placed = (
        P("cam", "sp", None),
        P("cam", "sp", None),
        P("cam", "sp", None),
        P("cam", "sp", None),
        P(),
        P(),
    )
    return jax.shard_map(
        local, mesh=mesh, in_specs=placed, out_specs=P("cam", "sp", None), check_vma=False
    )
```

profile of v0, /device:TPU:1, one launch (start us, length us, event | category | flops | bytes accessed | tf_op | source)
XLA Modules:
  0.0 154.9 jit_solution(5644704901470905810)
XLA Ops:
  0.0 1.7 %copy.28 = bf16[16,4,8,128]{3,2,1,0:T(8,128)(2,1)} copy(bf16[16,4,8,128]{3,2,0,1:T(8,128)(2,1)} %bitcast.112) | data formatting | bytes 262144 | tf_op jit(solution)/shard_map/transpose | solution.py:83
  1.7 17.8 %all-to-all-start.1 = ((bf16[64,8,128]{2,1,0:T(8,128)(2,1)}), bf16[64,8,128]{2,1,0:T(8,128)(2,1)S(1)}, u32[]{:S(2)}, u32[]{:S(2)}) async-start(bf16[64,8,128]{2,1,0:T(8,128)(2,1)} %bitcast.15), calls=%async_computation.1 | async-start | bytes 262144 | tf_op jit(solution)/shard_map/all_to_all | solution.py:93
  19.4 0.7 copy.29
  20.1 12.4 %all-to-all-done.1 = bf16[64,8,128]{2,1,0:T(8,128)(2,1)S(1)} async-done(((bf16[64,8,128]{2,1,0:T(8,128)(2,1)}), bf16[64,8,128]{2,1,0:T(8,128)(2,1)S(1)}, u32[]{:S(2)}, u32[]{:S(2)}) %all-to-all-start.1) | async-done | bytes 131104 | tf_op jit(solution)/shard_map/all_to_all | solution.py:93
  32.5 4.6 %all-to-all-start.2 = ((bf16[64,8,128]{2,1,0:T(8,128)(2,1)}), bf16[64,8,128]{2,1,0:T(8,128)(2,1)S(1)}, u32[]{:S(2)}, u32[]{:S(2)}) async-start(bf16[64,8,128]{2,1,0:T(8,128)(2,1)} %bitcast.19), calls=%async_computation.2 | async-start | bytes 262144 | tf_op jit(solution)/shard_map/all_to_all | solution.py:94
  37.2 13.4 %all-to-all-done.2 = bf16[64,8,128]{2,1,0:T(8,128)(2,1)S(1)} async-done(((bf16[64,8,128]{2,1,0:T(8,128)(2,1)}), bf16[64,8,128]{2,1,0:T(8,128)(2,1)S(1)}, u32[]{:S(2)}, u32[]{:S(2)}) %all-to-all-start.2) | async-done | bytes 131104 | tf_op jit(solution)/shard_map/all_to_all | solution.py:94
  50.6 0.9 broadcast_in_dim.18
  51.5 4.5 %all-to-all-start = ((bf16[64,32,128]{2,1,0:T(8,128)(2,1)}), bf16[64,32,128]{2,1,0:T(8,128)(2,1)S(1)}, u32[]{:S(2)}, u32[]{:S(2)}) async-start(bf16[64,32,128]{2,1,0:T(8,128)(2,1)} %bitcast.11), calls=%async_computation | async-start | bytes 1048576 | tf_op jit(solution)/shard_map/all_to_all | solution.py:90
  56.0 19.6 %all-to-all-done = bf16[64,32,128]{2,1,0:T(8,128)(2,1)S(1)} async-done(((bf16[64,32,128]{2,1,0:T(8,128)(2,1)}), bf16[64,32,128]{2,1,0:T(8,128)(2,1)S(1)}, u32[]{:S(2)}, u32[]{:S(2)}) %all-to-all-start) | async-done | bytes 524320 | tf_op jit(solution)/shard_map/all_to_all | solution.py:90
  75.6 6.8 %while.14 = (s32[]{:T(128)}, f32[4,512,128]{2,1,0:T(8,128)}, f32[4,512]{1,0:T(4,128)S(1)}, f32[4,512]{1,0:T(4,128)S(1)}, bf16[4,512,128]{2,1,0:T(8,128)(2,1)S(1)...) while((s32[]{:T(128)}, f32[4,512,128]{2,1,0:T(8,128)}, ...), condition=%wide.region_3.0_spmd, body=%wide.region_0.3_spmd.sunk | while | flops 135857664 | bytes 3830377 | solution.py:57
  75.6 0.3 fusion.42
  75.9 0.2 fusion.44
  76.1 0.1 dynamic_update_slice.17
  76.2 1.0 fusion.43
  77.3 0.3 fusion.42
  77.6 0.2 fusion.44
  77.8 0.1 dynamic_update_slice.17
  77.9 1.0 fusion.43
  79.0 0.3 fusion.42
  79.3 0.2 fusion.44
  79.5 0.1 dynamic_update_slice.17
  79.6 1.0 fusion.43
  80.7 0.3 fusion.42
  81.0 0.2 fusion.44
  81.2 0.1 dynamic_update_slice.17
  81.3 1.0 fusion.43
  82.3 0.7 all_to_all.46
  83.0 5.9 %all-to-all-start.4 = ((f32[64,1,32]{2,1,0:T(1,128)}), f32[64,1,32]{2,1,0:T(1,128)S(1)}, u32[]{:S(2)}, u32[]{:S(2)}) async-start(f32[64,1,32]{2,1,0:T(1,128)} %bitcast.23), calls=%async_computation.4 | async-start | bytes 65536 | tf_op jit(solution)/shard_map/all_to_all | solution.py:106
  88.9 0.1 all_to_all.48
  89.0 11.6 %all-to-all-done.4 = f32[64,1,32]{2,1,0:T(1,128)S(1)} async-done(((f32[64,1,32]{2,1,0:T(1,128)}), f32[64,1,32]{2,1,0:T(1,128)S(1)}, u32[]{:S(2)}, u32[]{:S(2)}) %all-to-all-start.4) | async-done | bytes 8224 | tf_op jit(solution)/shard_map/all_to_all | solution.py:106
  100.6 15.8 %all_to_all.56 = f32[64,1,32]{2,1,0:T(1,128)S(1)} all-to-all(f32[64,1,32]{2,1,0:T(1,128)S(1)} %bitcast.109), channel_id=1, replica_groups=mesh['cam'=8,'sp'=64] {'sp'}, dimensions={0} | all-to-all | bytes 16384 | tf_op jit(solution)/shard_map/all_to_all | solution.py:109
  116.4 4.9 %all-to-all-start.3 = ((f32[64,32,128]{2,1,0:T(8,128)}), f32[64,32,128]{2,1,0:T(8,128)S(1)}, u32[]{:S(2)}, u32[]{:S(2)}) async-start(f32[64,32,128]{2,1,0:T(8,128)} %bitcast.106), calls=%async_computation.3 | async-start | bytes 2097152 | tf_op jit(solution)/shard_map/all_to_all | solution.py:99
  121.3 3.1 %collective-permute-start.2 = (bf16[32,2048]{1,0:T(8,128)(2,1)S(1)}, bf16[32,2048]{1,0:T(8,128)(2,1)S(1)}, u32[]{:S(2)}, u32[]{:S(2)}) collective-permute-start(bf16[32,2048]{1,0:T(8,128)(2,1)S(1)} %bitcast.113), channel_id=1, source_target_pairs={{0,64},{64,128},{128,192},{192,256},{256,320},{320,384},{384,448},... | collective-permute-start | bytes 393224 | tf_op jit(solution)/shard_map/ppermute | solution.py:13
  124.4 4.3 %collective-permute-start.3 = (bf16[32,2048]{1,0:T(8,128)(2,1)S(1)}, bf16[32,2048]{1,0:T(8,128)(2,1)S(1)}, u32[]{:S(2)}, u32[]{:S(2)}) collective-permute-start(bf16[32,2048]{1,0:T(8,128)(2,1)S(1)} %bitcast.114), channel_id=1, source_target_pairs={{0,448},{64,0},{128,64},{192,128},{256,192},{320,256},{384,320},{4... | collective-permute-start | bytes 393224 | tf_op jit(solution)/shard_map/ppermute | solution.py:13
  128.7 1.9 %collective-permute-start = (bf16[32,2048]{1,0:T(8,128)(2,1)S(1)}, bf16[32,2048]{1,0:T(8,128)(2,1)S(1)}, u32[]{:S(2)}, u32[]{:S(2)}) collective-permute-start(bf16[32,2048]{1,0:T(8,128)(2,1)S(1)} %bitcast.116), channel_id=1, source_target_pairs={{0,64},{64,128},{128,192},{192,256},{256,320},{320,384},{384,448},... | collective-permute-start | bytes 393224 | tf_op jit(solution)/shard_map/ppermute | solution.py:13
  130.7 5.5 %collective-permute-start.1 = (bf16[32,2048]{1,0:T(8,128)(2,1)S(1)}, bf16[32,2048]{1,0:T(8,128)(2,1)S(1)}, u32[]{:S(2)}, u32[]{:S(2)}) collective-permute-start(bf16[32,2048]{1,0:T(8,128)(2,1)S(1)} %bitcast.117), channel_id=1, source_target_pairs={{0,448},{64,0},{128,64},{192,128},{256,192},{320,256},{384,320},{4... | collective-permute-start | bytes 393224 | tf_op jit(solution)/shard_map/ppermute | solution.py:13
  136.8 0.9 fusion.13
  137.8 12.3 %collective-permute-done.2 = bf16[32,2048]{1,0:T(8,128)(2,1)S(1)} collective-permute-done((bf16[32,2048]{1,0:T(8,128)(2,1)S(1)}, bf16[32,2048]{1,0:T(8,128)(2,1)S(1)}, u32[]{:S(2)}, u32[]{:S(2)}) %collective-permute-start.2) | collective-permute-done | bytes 131104 | tf_op jit(solution)/shard_map/ppermute | solution.py:13
  150.1 0.3 fusion.33
  150.4 0.3 fusion.20
  150.7 2.2 %collective-permute-done = bf16[32,2048]{1,0:T(8,128)(2,1)S(1)} collective-permute-done((bf16[32,2048]{1,0:T(8,128)(2,1)S(1)}, bf16[32,2048]{1,0:T(8,128)(2,1)S(1)}, u32[]{:S(2)}, u32[]{:S(2)}) %collective-permute-start) | collective-permute-done | bytes 131104 | tf_op jit(solution)/shard_map/ppermute | solution.py:13
  152.9 0.3 fusion.11
  153.2 0.2 copy.36
  153.4 0.1 multiply_reduce_fusion.1
  153.5 0.3 multiply_reduce_fusion
  153.8 0.1 fusion.23
  153.9 0.2 copy.32
  154.2 0.7 add_convert_fusion
  (35 shorter events, 0.4 us)
Async XLA Ops:
  0.0 136.8 %copy-start = (f32[50,2,2048]{2,1,0:T(2,128)S(1)}, f32[50,2,2048]{2,1,0:T(2,128)}, u32[]{:S(2)}) copy-start(f32[50,2,2048]{2,1,0:T(2,128)} %param.13) | copy-start | bytes 2457604
  1.7 17.8 %copy-start.4 = (bf16[1,32,2048]{2,1,0:T(8,128)(2,1)S(1)}, bf16[1,32,2048]{2,1,0:T(8,128)(2,1)}, u32[]{:S(2)}) copy-start(bf16[1,32,2048]{2,1,0:T(8,128)(2,1)} %param.10) | copy-start | bytes 393220
  1.7 30.9 %all-to-all-start.1 = ((bf16[64,8,128]{2,1,0:T(8,128)(2,1)}), bf16[64,8,128]{2,1,0:T(8,128)(2,1)S(1)}, u32[]{:S(2)}, u32[]{:S(2)}) async-start(bf16[64,8,128]{2,1,0:T(8,128)(2,1)} %bitcast.15), calls=%async_computation.1 | async-start | bytes 262144 | tf_op jit(solution)/shard_map/all_to_all | solution.py:93
  32.5 4.6 %copy-start.1 = (bf16[1,32,2048]{2,1,0:T(8,128)(2,1)S(1)}, bf16[1,32,2048]{2,1,0:T(8,128)(2,1)}, u32[]{:S(2)}) copy-start(bf16[1,32,2048]{2,1,0:T(8,128)(2,1)} %param.8) | copy-start | bytes 393220
  32.5 18.0 %all-to-all-start.2 = ((bf16[64,8,128]{2,1,0:T(8,128)(2,1)}), bf16[64,8,128]{2,1,0:T(8,128)(2,1)S(1)}, u32[]{:S(2)}, u32[]{:S(2)}) async-start(bf16[64,8,128]{2,1,0:T(8,128)(2,1)} %bitcast.19), calls=%async_computation.2 | async-start | bytes 262144 | tf_op jit(solution)/shard_map/all_to_all | solution.py:94
  51.5 24.1 %all-to-all-start = ((bf16[64,32,128]{2,1,0:T(8,128)(2,1)}), bf16[64,32,128]{2,1,0:T(8,128)(2,1)S(1)}, u32[]{:S(2)}, u32[]{:S(2)}) async-start(bf16[64,32,128]{2,1,0:T(8,128)(2,1)} %bitcast.11), calls=%async_computation | async-start | bytes 1048576 | tf_op jit(solution)/shard_map/all_to_all | solution.py:90
  83.0 17.6 %all-to-all-start.4 = ((f32[64,1,32]{2,1,0:T(1,128)}), f32[64,1,32]{2,1,0:T(1,128)S(1)}, u32[]{:S(2)}, u32[]{:S(2)}) async-start(f32[64,1,32]{2,1,0:T(1,128)} %bitcast.23), calls=%async_computation.4 | async-start | bytes 65536 | tf_op jit(solution)/shard_map/all_to_all | solution.py:106
  116.4 4.9 %copy-start.3 = (bf16[1,32,2048]{2,1,0:T(8,128)(2,1)S(1)}, bf16[1,32,2048]{2,1,0:T(8,128)(2,1)}, u32[]{:S(2)}) copy-start(bf16[1,32,2048]{2,1,0:T(8,128)(2,1)} %param.9) | copy-start | bytes 393220
  116.4 37.0 %all-to-all-start.3 = ((f32[64,32,128]{2,1,0:T(8,128)}), f32[64,32,128]{2,1,0:T(8,128)S(1)}, u32[]{:S(2)}, u32[]{:S(2)}) async-start(f32[64,32,128]{2,1,0:T(8,128)} %bitcast.106), calls=%async_computation.3 | async-start | bytes 2097152 | tf_op jit(solution)/shard_map/all_to_all | solution.py:99
  121.3 28.8 %collective-permute-start.2 = (bf16[32,2048]{1,0:T(8,128)(2,1)S(1)}, bf16[32,2048]{1,0:T(8,128)(2,1)S(1)}, u32[]{:S(2)}, u32[]{:S(2)}) collective-permute-start(bf16[32,2048]{1,0:T(8,128)(2,1)S(1)} %bitcast.113), channel_id=1, source_target_pairs={{0,64},{64,128},{128,192},{192,256},{256,320},{320,384},{384,448},... | collective-permute-start | bytes 393224 | tf_op jit(solution)/shard_map/ppermute | solution.py:13
  124.4 25.6 %collective-permute-start.3 = (bf16[32,2048]{1,0:T(8,128)(2,1)S(1)}, bf16[32,2048]{1,0:T(8,128)(2,1)S(1)}, u32[]{:S(2)}, u32[]{:S(2)}) collective-permute-start(bf16[32,2048]{1,0:T(8,128)(2,1)S(1)} %bitcast.114), channel_id=1, source_target_pairs={{0,448},{64,0},{128,64},{192,128},{256,192},{320,256},{384,320},{4... | collective-permute-start | bytes 393224 | tf_op jit(solution)/shard_map/ppermute | solution.py:13
  128.7 24.2 %collective-permute-start = (bf16[32,2048]{1,0:T(8,128)(2,1)S(1)}, bf16[32,2048]{1,0:T(8,128)(2,1)S(1)}, u32[]{:S(2)}, u32[]{:S(2)}) collective-permute-start(bf16[32,2048]{1,0:T(8,128)(2,1)S(1)} %bitcast.116), channel_id=1, source_target_pairs={{0,64},{64,128},{128,192},{192,256},{256,320},{320,384},{384,448},... | collective-permute-start | bytes 393224 | tf_op jit(solution)/shard_map/ppermute | solution.py:13
  130.7 22.2 %collective-permute-start.1 = (bf16[32,2048]{1,0:T(8,128)(2,1)S(1)}, bf16[32,2048]{1,0:T(8,128)(2,1)S(1)}, u32[]{:S(2)}, u32[]{:S(2)}) collective-permute-start(bf16[32,2048]{1,0:T(8,128)(2,1)S(1)} %bitcast.117), channel_id=1, source_target_pairs={{0,448},{64,0},{128,64},{192,128},{256,192},{320,256},{384,320},{4... | collective-permute-start | bytes 393224 | tf_op jit(solution)/shard_map/ppermute | solution.py:13
  136.8 0.9 copy-start.2
where the time goes:
time: 156 us; the launch traced here: 155 us
  waiting for transfers between devices  71.6 us (46%)
  starting transfers between devices  52.3 us (34%)
  blocking collectives  15.8 us (10%)
  matrix products  6.9 us (4%)
  local copies, waits for them, and re-layouts  4.86 us (3%)
  other arithmetic  2.36 us (2%)
    all_to_all x1, waiting for transfers between devices, local(): lax.all_to_all(spread.reshape(groups, row_count, head_dim), 'sp', split_a...  19.6 us
    all_to_all x1, starting transfers between devices, local(): lax.all_to_all(quartered(key_heads), 'sp', split_axis=0, concat_axis=1, t...  17.8 us
    all_to_all x1, blocking collectives, local(): lax.all_to_all(totals.reshape(groups, row_count), 'sp', split_axis=0, con...  15.8 us
    ppermute x4, starting transfers between devices, passed_along(): return lax.ppermute(value, axis, pairs)  14.8 us
    ppermute x4, waiting for transfers between devices, passed_along(): return lax.ppermute(value, axis, pairs)  14.5 us
    all_to_all x1, waiting for transfers between devices, local(): lax.all_to_all(quartered(value_heads), 'sp', split_axis=0, concat_axis=1,...  13.4 us
    all_to_all x1, waiting for transfers between devices, local(): lax.all_to_all(quartered(key_heads), 'sp', split_axis=0, concat_axis=1, t...  12.4 us
    all_to_all x1, waiting for transfers between devices, local(): lax.all_to_all(runmax.reshape(groups, row_count), 'sp', split_axis=0, con...  11.6 us
  transfers between devices with their start and end apart: 9, of which 6 were waited for; matrix products, arithmetic and copies ran while one was open for 2% of the time, Pallas kernels for 0%

commit v1 on v0

--- a/solution.py
+++ b/solution.py
@@ -87,9 +87,16 @@
     spread = jnp.broadcast_to(
         query_heads.transpose(1, 0, 2)[:, None], (head_count, copies, row_count, head_dim)
     )
-    queries_here = lax.all_to_all(
-        spread.reshape(groups, row_count, head_dim), "sp", split_axis=0, concat_axis=1, tiled=True
+    choose_squares = lambda w_in, shard_axis: jnp.concatenate(
+        lax.all_to_all(
+            jnp.stack(jnp.split(w_in, lax.axis_size(shard_axis), 0)),
+            concat_axis=0,
+            split_axis=0,
+            axis_name=shard_axis,
+        ),
+        1,
     )
+    queries_here = choose_squares(spread.reshape(groups, row_count, head_dim), "sp")
     keys_here = lax.all_to_all(quartered(key_heads), "sp", split_axis=0, concat_axis=1, tiled=True)
     values_here = lax.all_to_all(
         quartered(value_heads), "sp", split_axis=0, concat_axis=1, tiled=True

time: 156 us -> 188 us (1.21)
  local copies, waits for them, and re-layouts: 4.86 us -> 42.1 us
  waiting for transfers between devices: 71.6 us -> 57.7 us
  starting transfers between devices: 52.3 us -> 60.7 us
    unnamed x12 -> x75, local copies, waits for them, and re-layouts: 0.06 us -> 37.5 us
    all_to_all x1, waiting for transfers between devices: 12.4 us -> 0.01 us  [local(): lax.all_to_all(quartered(key_heads), 'sp', split_axis=0, concat_axis=1, t...]
    all_to_all x1, starting transfers between devices: 4.57 us -> 12.7 us  [local(): lax.all_to_all(quartered(value_heads), 'sp', split_axis=0, concat_axis=1,...]
  transfers between devices with their start and end apart: 9 -> 9, of which waited for: 6 -> 5; matrix products, arithmetic and copies ran while one was open for 2% -> 22% of each run, Pallas kernels for 0% -> 0%
where the time goes in v1:
time: 188 us; the launch traced here: 187 us
  starting transfers between devices  60.7 us (32%)
  waiting for transfers between devices  57.7 us (31%)
  local copies, waits for them, and re-layouts  42.1 us (22%)
  blocking collectives  15.8 us (8%)
  matrix products  6.89 us (4%)
  other arithmetic  2.36 us (1%)
    unnamed x75, local copies, waits for them, and re-layouts  37.5 us
    all_to_all x1, waiting for transfers between devices, local(): lax.all_to_all(jnp.stack(jnp.split(w_in, lax.axis_size(shard_axis), 0)),...  19.3 us
    all_to_all x1, starting transfers between devices, local(): lax.all_to_all(quartered(key_heads), 'sp', split_axis=0, concat_axis=1, t...  17.8 us
    all_to_all x1, blocking collectives, local(): lax.all_to_all(totals.reshape(groups, row_count), 'sp', split_axis=0, con...  15.8 us
    ppermute x4, waiting for transfers between devices, passed_along(): return lax.ppermute(value, axis, pairs)  14.8 us
    ppermute x4, starting transfers between devices, passed_along(): return lax.ppermute(value, axis, pairs)  14.8 us
    all_to_all x1, starting transfers between devices, local(): lax.all_to_all(quartered(value_heads), 'sp', split_axis=0, concat_axis=1,...  12.7 us
    all_to_all x1, waiting for transfers between devices, local(): lax.all_to_all(quartered(value_heads), 'sp', split_axis=0, concat_axis=1,...  11.9 us
  transfers between devices with their start and end apart: 9, of which 5 were waited for; matrix products, arithmetic and copies ran while one was open for 22% of the time, Pallas kernels for 0%

profile of v1, /device:TPU:1, one launch (start us, length us, event | category | flops | bytes accessed | tf_op | source)
XLA Modules:
  0.0 186.7 jit_solution(7588343600462875545)
XLA Ops:
  0.0 1.7 copy.154
  1.7 17.8 %all-to-all-start.1 = ((bf16[64,8,128]{2,1,0:T(8,128)(2,1)}), bf16[64,8,128]{2,1,0:T(8,128)(2,1)S(1)}, u32[]{:S(2)}, u32[]{:S(2)}) async-start(bf16[64,8,128]{2,1,0:T(8,128)(2,1)} %bitcast.79), calls=%async_computation.1 | async-start | bytes 262144 | tf_op jit(solution)/shard_map/all_to_all | solution.py:100
  19.6 0.6 constant_dynamic-update-slice_fusion.63
  20.2 0.6 constant_dynamic-update-slice_fusion.62
  20.8 0.6 constant_dynamic-update-slice_fusion.61
  22.6 0.6 constant_dynamic-update-slice_fusion.58
  23.8 0.6 constant_dynamic-update-slice_fusion.56
  26.7 0.6 constant_dynamic-update-slice_fusion.51
  28.5 0.6 constant_dynamic-update-slice_fusion.48
  32.1 0.6 constant_dynamic-update-slice_fusion.42
  33.9 0.6 constant_dynamic-update-slice_fusion.39
  36.9 0.6 constant_dynamic-update-slice_fusion.34
  38.1 0.6 constant_dynamic-update-slice_fusion.32
  39.2 0.6 constant_dynamic-update-slice_fusion.30
  39.8 0.6 constant_dynamic-update-slice_fusion.29
  41.0 0.6 constant_dynamic-update-slice_fusion.27
  41.6 0.6 constant_dynamic-update-slice_fusion.26
  44.0 0.6 constant_dynamic-update-slice_fusion.22
  47.6 0.6 constant_dynamic-update-slice_fusion.16
  48.2 0.6 constant_dynamic-update-slice_fusion.15
  51.2 0.6 constant_dynamic-update-slice_fusion.10
  52.3 0.6 constant_dynamic-update-slice_fusion.8
  52.9 0.6 constant_dynamic-update-slice_fusion.7
  54.1 0.6 constant_dynamic-update-slice_fusion.5
  55.3 0.6 constant_dynamic-update-slice_fusion.3
  55.9 0.7 copy.155
  57.2 12.7 %all-to-all-start.2 = ((bf16[64,8,128]{2,1,0:T(8,128)(2,1)}), bf16[64,8,128]{2,1,0:T(8,128)(2,1)S(1)}, u32[]{:S(2)}, u32[]{:S(2)}) async-start(bf16[64,8,128]{2,1,0:T(8,128)(2,1)} %bitcast.83), calls=%async_computation.2 | async-start | bytes 262144 | tf_op jit(solution)/shard_map/all_to_all | solution.py:101
  71.1 11.9 %all-to-all-done.2 = bf16[64,8,128]{2,1,0:T(8,128)(2,1)S(1)} async-done(((bf16[64,8,128]{2,1,0:T(8,128)(2,1)}), bf16[64,8,128]{2,1,0:T(8,128)(2,1)S(1)}, u32[]{:S(2)}, u32[]{:S(2)}) %all-to-all-start.2) | async-done | bytes 131104 | tf_op jit(solution)/shard_map/all_to_all | solution.py:101
  83.0 4.5 %all-to-all-start = ((bf16[64,1,32,128]{3,2,1,0:T(8,128)(2,1)}), bf16[64,1,32,128]{3,2,1,0:T(8,128)(2,1)S(1)}, u32[]{:S(2)}, u32[]{:S(2)}) async-start(bf16[64,1,32,128]{3,2,1,0:T(8,128)(2,1)} %constant_dynamic-update-slice_fusion), calls=%async_computation | async-start | bytes 1048576 | tf_op jit(solution)/shard_map/all_to_all | solution.py:91
  87.5 19.3 %all-to-all-done = bf16[64,1,32,128]{3,2,1,0:T(8,128)(2,1)S(1)} async-done(((bf16[64,1,32,128]{3,2,1,0:T(8,128)(2,1)}), bf16[64,1,32,128]{3,2,1,0:T(8,128)(2,1)S(1)}, u32[]{:S(2)}, u32[]{:S(2)}) %all-to-all-start) | async-done | bytes 524320 | tf_op jit(solution)/shard_map/all_to_all | solution.py:91
  106.9 6.8 %while.14 = (s32[]{:T(128)}, f32[4,512,128]{2,1,0:T(8,128)}, f32[4,512]{1,0:T(4,128)S(1)}, f32[4,512]{1,0:T(4,128)S(1)}, bf16[4,512,128]{2,1,0:T(8,128)(2,1)S(1)...) while((s32[]{:T(128)}, f32[4,512,128]{2,1,0:T(8,128)}, ...), condition=%wide.region_3.0_spmd, body=%wide.region_0.3_spmd.sunk | while | flops 135857664 | bytes 3830377 | solution.py:57
  107.5 1.0 fusion.43
  109.2 1.0 fusion.43
  110.9 1.0 fusion.43
  112.6 1.0 fusion.43
  113.6 0.7 all_to_all.42
  114.3 6.1 %all-to-all-start.4 = ((f32[64,1,32]{2,1,0:T(1,128)}), f32[64,1,32]{2,1,0:T(1,128)S(1)}, u32[]{:S(2)}, u32[]{:S(2)}) async-start(f32[64,1,32]{2,1,0:T(1,128)} %bitcast.87), calls=%async_computation.4 | async-start | bytes 65536 | tf_op jit(solution)/shard_map/all_to_all | solution.py:113
  120.5 11.7 %all-to-all-done.4 = f32[64,1,32]{2,1,0:T(1,128)S(1)} async-done(((f32[64,1,32]{2,1,0:T(1,128)}), f32[64,1,32]{2,1,0:T(1,128)S(1)}, u32[]{:S(2)}, u32[]{:S(2)}) %all-to-all-start.4) | async-done | bytes 8224 | tf_op jit(solution)/shard_map/all_to_all | solution.py:113
  132.2 15.8 %all_to_all.52 = f32[64,1,32]{2,1,0:T(1,128)S(1)} all-to-all(f32[64,1,32]{2,1,0:T(1,128)S(1)} %bitcast.429), channel_id=1, replica_groups=mesh['cam'=8,'sp'=64] {'sp'}, dimensions={0} | all-to-all | bytes 16384 | tf_op jit(solution)/shard_map/all_to_all | solution.py:116
  148.0 4.9 %all-to-all-start.3 = ((f32[64,32,128]{2,1,0:T(8,128)}), f32[64,32,128]{2,1,0:T(8,128)S(1)}, u32[]{:S(2)}, u32[]{:S(2)}) async-start(f32[64,32,128]{2,1,0:T(8,128)} %bitcast.426), calls=%async_computation.3 | async-start | bytes 2097152 | tf_op jit(solution)/shard_map/all_to_all | solution.py:106
  152.9 3.1 %collective-permute-start.2 = (bf16[32,2048]{1,0:T(8,128)(2,1)S(1)}, bf16[32,2048]{1,0:T(8,128)(2,1)S(1)}, u32[]{:S(2)}, u32[]{:S(2)}) collective-permute-start(bf16[32,2048]{1,0:T(8,128)(2,1)S(1)} %bitcast.433), channel_id=1, source_target_pairs={{0,64},{64,128},{128,192},{192,256},{256,320},{320,384},{384,448},... | collective-permute-start | bytes 393224 | tf_op jit(solution)/shard_map/ppermute | solution.py:13
  156.0 4.3 %collective-permute-start.3 = (bf16[32,2048]{1,0:T(8,128)(2,1)S(1)}, bf16[32,2048]{1,0:T(8,128)(2,1)S(1)}, u32[]{:S(2)}, u32[]{:S(2)}) collective-permute-start(bf16[32,2048]{1,0:T(8,128)(2,1)S(1)} %bitcast.434), channel_id=1, source_target_pairs={{0,448},{64,0},{128,64},{192,128},{256,192},{320,256},{384,320},{4... | collective-permute-start | bytes 393224 | tf_op jit(solution)/shard_map/ppermute | solution.py:13
  160.3 1.9 %collective-permute-start = (bf16[32,2048]{1,0:T(8,128)(2,1)S(1)}, bf16[32,2048]{1,0:T(8,128)(2,1)S(1)}, u32[]{:S(2)}, u32[]{:S(2)}) collective-permute-start(bf16[32,2048]{1,0:T(8,128)(2,1)S(1)} %bitcast.436), channel_id=1, source_target_pairs={{0,64},{64,128},{128,192},{192,256},{256,320},{320,384},{384,448},... | collective-permute-start | bytes 393224 | tf_op jit(solution)/shard_map/ppermute | solution.py:13
  162.2 5.5 %collective-permute-start.1 = (bf16[32,2048]{1,0:T(8,128)(2,1)S(1)}, bf16[32,2048]{1,0:T(8,128)(2,1)S(1)}, u32[]{:S(2)}, u32[]{:S(2)}) collective-permute-start(bf16[32,2048]{1,0:T(8,128)(2,1)S(1)} %bitcast.437), channel_id=1, source_target_pairs={{0,448},{64,0},{128,64},{192,128},{256,192},{320,256},{384,320},{4... | collective-permute-start | bytes 393224 | tf_op jit(solution)/shard_map/ppermute | solution.py:13
  168.4 0.9 fusion.13
  169.3 12.6 %collective-permute-done.2 = bf16[32,2048]{1,0:T(8,128)(2,1)S(1)} collective-permute-done((bf16[32,2048]{1,0:T(8,128)(2,1)S(1)}, bf16[32,2048]{1,0:T(8,128)(2,1)S(1)}, u32[]{:S(2)}, u32[]{:S(2)}) %collective-permute-start.2) | collective-permute-done | bytes 131104 | tf_op jit(solution)/shard_map/ppermute | solution.py:13
  182.5 2.2 %collective-permute-done = bf16[32,2048]{1,0:T(8,128)(2,1)S(1)} collective-permute-done((bf16[32,2048]{1,0:T(8,128)(2,1)S(1)}, bf16[32,2048]{1,0:T(8,128)(2,1)S(1)}, u32[]{:S(2)}, u32[]{:S(2)}) %collective-permute-start) | collective-permute-done | bytes 131104 | tf_op jit(solution)/shard_map/ppermute | solution.py:13
  186.0 0.7 add_convert_fusion
  (99 shorter events, 28.9 us)
Async XLA Ops:
  0.0 168.4 %copy-start = (f32[50,2,2048]{2,1,0:T(2,128)S(1)}, f32[50,2,2048]{2,1,0:T(2,128)}, u32[]{:S(2)}) copy-start(f32[50,2,2048]{2,1,0:T(2,128)} %param.13) | copy-start | bytes 2457604
  1.7 17.8 %copy-start.1 = (bf16[1,32,2048]{2,1,0:T(8,128)(2,1)S(1)}, bf16[1,32,2048]{2,1,0:T(8,128)(2,1)}, u32[]{:S(2)}) copy-start(bf16[1,32,2048]{2,1,0:T(8,128)(2,1)} %param.8) | copy-start | bytes 393220
  1.7 55.5 %all-to-all-start.1 = ((bf16[64,8,128]{2,1,0:T(8,128)(2,1)}), bf16[64,8,128]{2,1,0:T(8,128)(2,1)S(1)}, u32[]{:S(2)}, u32[]{:S(2)}) async-start(bf16[64,8,128]{2,1,0:T(8,128)(2,1)} %bitcast.79), calls=%async_computation.1 | async-start | bytes 262144 | tf_op jit(solution)/shard_map/all_to_all | solution.py:100
  46.4 9.5 %copy-start.4 = (bf16[1,32,2048]{2,1,0:T(8,128)(2,1)S(1)}, bf16[1,32,2048]{2,1,0:T(8,128)(2,1)}, u32[]{:S(2)}) copy-start(bf16[1,32,2048]{2,1,0:T(8,128)(2,1)} %param.10) | copy-start | bytes 393220
  57.2 25.8 %all-to-all-start.2 = ((bf16[64,8,128]{2,1,0:T(8,128)(2,1)}), bf16[64,8,128]{2,1,0:T(8,128)(2,1)S(1)}, u32[]{:S(2)}, u32[]{:S(2)}) async-start(bf16[64,8,128]{2,1,0:T(8,128)(2,1)} %bitcast.83), calls=%async_computation.2 | async-start | bytes 262144 | tf_op jit(solution)/shard_map/all_to_all | solution.py:101
  83.0 23.9 %all-to-all-start = ((bf16[64,1,32,128]{3,2,1,0:T(8,128)(2,1)}), bf16[64,1,32,128]{3,2,1,0:T(8,128)(2,1)S(1)}, u32[]{:S(2)}, u32[]{:S(2)}) async-start(bf16[64,1,32,128]{3,2,1,0:T(8,128)(2,1)} %constant_dynamic-update-slice_fusion), calls=%async_computation | async-start | bytes 1048576 | tf_op jit(solution)/shard_map/all_to_all | solution.py:91
  114.3 17.8 %all-to-all-start.4 = ((f32[64,1,32]{2,1,0:T(1,128)}), f32[64,1,32]{2,1,0:T(1,128)S(1)}, u32[]{:S(2)}, u32[]{:S(2)}) async-start(f32[64,1,32]{2,1,0:T(1,128)} %bitcast.87), calls=%async_computation.4 | async-start | bytes 65536 | tf_op jit(solution)/shard_map/all_to_all | solution.py:113
  148.0 4.9 %copy-start.3 = (bf16[1,32,2048]{2,1,0:T(8,128)(2,1)S(1)}, bf16[1,32,2048]{2,1,0:T(8,128)(2,1)}, u32[]{:S(2)}) copy-start(bf16[1,32,2048]{2,1,0:T(8,128)(2,1)} %param.9) | copy-start | bytes 393220
  148.0 37.3 %all-to-all-start.3 = ((f32[64,32,128]{2,1,0:T(8,128)}), f32[64,32,128]{2,1,0:T(8,128)S(1)}, u32[]{:S(2)}, u32[]{:S(2)}) async-start(f32[64,32,128]{2,1,0:T(8,128)} %bitcast.426), calls=%async_computation.3 | async-start | bytes 2097152 | tf_op jit(solution)/shard_map/all_to_all | solution.py:106
  152.9 29.0 %collective-permute-start.2 = (bf16[32,2048]{1,0:T(8,128)(2,1)S(1)}, bf16[32,2048]{1,0:T(8,128)(2,1)S(1)}, u32[]{:S(2)}, u32[]{:S(2)}) collective-permute-start(bf16[32,2048]{1,0:T(8,128)(2,1)S(1)} %bitcast.433), channel_id=1, source_target_pairs={{0,64},{64,128},{128,192},{192,256},{256,320},{320,384},{384,448},... | collective-permute-start | bytes 393224 | tf_op jit(solution)/shard_map/ppermute | solution.py:13
  156.0 25.9 %collective-permute-start.3 = (bf16[32,2048]{1,0:T(8,128)(2,1)S(1)}, bf16[32,2048]{1,0:T(8,128)(2,1)S(1)}, u32[]{:S(2)}, u32[]{:S(2)}) collective-permute-start(bf16[32,2048]{1,0:T(8,128)(2,1)S(1)} %bitcast.434), channel_id=1, source_target_pairs={{0,448},{64,0},{128,64},{192,128},{256,192},{320,256},{384,320},{4... | collective-permute-start | bytes 393224 | tf_op jit(solution)/shard_map/ppermute | solution.py:13
  160.3 24.4 %collective-permute-start = (bf16[32,2048]{1,0:T(8,128)(2,1)S(1)}, bf16[32,2048]{1,0:T(8,128)(2,1)S(1)}, u32[]{:S(2)}, u32[]{:S(2)}) collective-permute-start(bf16[32,2048]{1,0:T(8,128)(2,1)S(1)} %bitcast.436), channel_id=1, source_target_pairs={{0,64},{64,128},{128,192},{192,256},{256,320},{320,384},{384,448},... | collective-permute-start | bytes 393224 | tf_op jit(solution)/shard_map/ppermute | solution.py:13
  162.2 22.5 %collective-permute-start.1 = (bf16[32,2048]{1,0:T(8,128)(2,1)S(1)}, bf16[32,2048]{1,0:T(8,128)(2,1)S(1)}, u32[]{:S(2)}, u32[]{:S(2)}) collective-permute-start(bf16[32,2048]{1,0:T(8,128)(2,1)S(1)} %bitcast.437), channel_id=1, source_target_pairs={{0,448},{64,0},{128,64},{192,128},{256,192},{320,256},{384,320},{4... | collective-permute-start | bytes 393224 | tf_op jit(solution)/shard_map/ppermute | solution.py:13
  168.4 0.9 copy-start.2
